TPU v7x, 128 devices: a whole 4x4x4 slice. The times are simulated.
128 devices in a mesh: token: 8 (over y, core), tensor: 16 (over z, x).
Axes of the slice: x: 4, y: 4, z: 4, core: 2. Of those that a mesh axis runs over, the one named last changes fastest.
Arguments:
- tokens: bfloat16 [8192, 4096], P(('token', 'tensor')), may hold values from -6 to 6
- doc_lengths: int32 [4], replicated, may hold values from 1 to 4096, 8192 in all
- attn_gain: float32 [4096], replicated, may hold values from 0.1 to 1.9
- mlp_gain: float32 [4096], replicated, may hold values from 0.1 to 1.9
- w_query: bfloat16 [4096, 4096], P(None, 'tensor'), may hold values from -0.067528728 to 0.067528728
- w_keyval: bfloat16 [4096, 2048], P(None, 'tensor'), may hold values from -0.067528728 to 0.067528728
- w_out: bfloat16 [4096, 4096], P('tensor'), may hold values from -0.09375 to 0.09375
- w_gate: bfloat16 [4096, 7168], P(None, 'tensor'), may hold values from -0.09375 to 0.09375
- w_up: bfloat16 [4096, 7168], P(None, 'tensor'), may hold values from -0.09375 to 0.09375
- w_down: bfloat16 [7168, 4096], P('tensor'), may hold values from -0.0625 to 0.0625
Outputs:
- layer_out: bfloat16 [8192, 4096], P(('token', 'tensor'))
Inputs may be any that keep to these rules, and one draw needn't show every extreme that they name: `doc_lengths`: the lengths sum to 8192; exactly one document has length 4096, the largest allowed.
All inputs are finite; a program needn't handle non-finite values.
Results may differ from a plain program's by a relative error of at most 0.017.
Values may be sent and summed in bfloat16 or wider, within the bound.
A program may use at most 128 MiB of HBM per device.

v0:
```python
import functools
import math

import jax
import jax.numpy as jnp
from jax import lax
from jax.experimental import pallas as pl
from jax.experimental.pallas import tpu as pltpu
from jax.sharding import PartitionSpec as P

HEAD_DIM = 128
SIDE = 4
CORES = 2
YS = 4

EPSILON = 1e-05
ROPE_BASE = 500000.0
NEGATIVE = -1e30
MESH = pl.DeviceIdType.MESH


def place():
    me, token = lax.axis_index("tensor"), lax.axis_index("token")
    return me // SIDE, me % SIDE, token // CORES, token % CORES


def along_z(step):
    z, x, _, _ = place()
    return {"tensor": ((z + step + SIDE) % SIDE) * SIDE + x}


def mate():
    z, x, _, _ = place()
    return {"tensor": z * SIDE + SIDE - 1 - x}


def holder():
    z, x, _, _ = place()
    return {"tensor": z * SIDE + x + 1 - 2 * (x % 2)}


def along_y(step):
    _, _, y, core = place()
    return {"token": ((y + step + YS) % YS) * CORES + core}


def twin():
    _, _, y, core = place()
    return {"token": y * CORES + 1 - core}


def greet():
    others = [along_z(1), along_z(-1), mate(), holder(), along_y(1), along_y(-1), twin()]
    for other in others:
        pl.semaphore_signal(pltpu.get_barrier_semaphore(), inc=1, device_id=other, device_id_type=MESH)
    return len(others)


def meet(others):
    pl.semaphore_wait(pltpu.get_barrier_semaphore(), others)


def column_halves(width):
    first = width * 9 // 16
    return first, width - first


class Wires:
    def __init__(self, send_sems, recv_sems):
        self.send_sems, self.recv_sems, self.slots, self.started = send_sems, recv_sems, {}, []

    def copy(self, key, src, dst, device):
        slot = self.slots.setdefault(key, len(self.slots))
        return pltpu.make_async_remote_copy(
            src_ref=src,
            dst_ref=dst,
            send_sem=self.send_sems.at[slot],
            recv_sem=self.recv_sems.at[slot],
            device_id=device,
            device_id_type=MESH,
        )

    def start(self, key, src, dst, device):
        made = self.copy(key, src, dst, device)
        made.start()
        self.started.append(made)

    def arrive(self, key, dst, device):
        self.copy(key, dst, dst, device).wait_recv()

    def drain(self):
        for made in self.started:
            made.wait_send()
        self.started = []


class Fetch:
    def __init__(self, wires, name, src, dst, lanes, first_lane=0):
        self.wires, self.name, self.src, self.dst, self.lanes, self.first_lane = wires, name, src, dst, lanes, first_lane
        self.size = src.shape[1 if lanes else 0] // (YS * CORES)

    def cut(self, ref, number, part, offset):
        size = self.size if part is None else self.size // 2
        start = pl.multiple_of(number * self.size, self.size) + (0 if part in (None, 0) else size)
        start = pl.multiple_of(start, size)
        if self.lanes:
            return ref.at[:, pl.ds(start, size)]
        return ref.at[pl.ds(start, size), pl.ds(offset, self.src.shape[1])]

    def slot(self, dy, dc, part=None):
        _, _, y, core = place()
        number = ((y + dy + YS) % YS) * CORES + (core if dc == 0 else 1 - core)
        return self.cut(self.dst, number, part, self.first_lane)

    def start(self, key, ref, device):
        self.wires.start((self.name, key), ref, ref, device)

    def arrive(self, key, ref):
        self.wires.arrive((self.name, key), ref, holder())

    def ask(self):
        _, _, y, core = place()
        self.wires.start((self.name, "x"), self.cut(self.src, y * CORES + core, None, 0), self.slot(0, 0), holder())

    def relay(self):
        self.arrive("x", self.slot(0, 0))
        self.start("y3", self.slot(0, 0), along_y(1))
        self.start("y1", self.slot(0, 0), along_y(-1))
        self.start("c0", self.slot(0, 0), twin())

    def pass_on(self):
        self.arrive("y3", self.slot(3, 0))
        self.start("h0", self.slot(3, 0, 0), along_y(1))
        self.start("c3", self.slot(3, 0), twin())
        self.arrive("y1", self.slot(1, 0))
        self.start("h1", self.slot(1, 0, 1), along_y(-1))
        self.start("c1", self.slot(1, 0), twin())

    def settle(self):
        self.arrive("h0", self.slot(2, 0, 0))
        self.arrive("h1", self.slot(2, 0, 1))
        self.start("c2", self.slot(2, 0), twin())

    def finish(self):
        for dy in (0, 3, 1, 2):
            self.arrive("c%d" % dy, self.slot(dy, 1))


def gather(wires, blocks, hook):
    rows = blocks[0].shape[2]
    low, high = pl.ds(0, rows // 2), pl.ds(rows // 2, rows // 2)
    up, down = 1, -1

    def full(h, dz, m):
        return blocks[h].at[dz, m]

    def spread(h, m):
        wires.start(("s", h, 3, m), full(h, 0, m), full(h, 3, m), along_z(up))
        wires.start(("s", h, 1, m), full(h, 0, m), full(h, 1, m), along_z(down))

    def to_mate(h, dz):
        wires.start(("m", h, dz), full(h, dz, 0), full(h, dz, 1), mate())

    def relay(h, m, onward):
        wires.arrive(("s", h, 3, m), full(h, 3, m), along_z(down))
        wires.start(("t", h, 0, m), blocks[h].at[3, m, low], blocks[h].at[2, m, low], along_z(up))
        if onward:
            to_mate(h, 3)
        wires.arrive(("s", h, 1, m), full(h, 1, m), along_z(up))
        wires.start(("t", h, 1, m), blocks[h].at[1, m, high], blocks[h].at[2, m, high], along_z(down))
        if onward:
            to_mate(h, 1)

    def last(h, m):
        wires.arrive(("t", h, 0, m), blocks[h].at[2, m, low], along_z(down))
        wires.arrive(("t", h, 1, m), blocks[h].at[2, m, high], along_z(up))

    to_mate(0, 0)
    spread(1, 0)
    spread(0, 0)
    to_mate(1, 0)
    hook("sent")
    wires.arrive(("m", 0, 0), full(0, 0, 1), mate())
    spread(0, 1)
    relay(1, 0, True)
    hook("one")
    relay(0, 0, False)
    wires.arrive(("m", 1, 0), full(1, 0, 1), mate())
    hook("own pair")
    last(1, 0)
    to_mate(1, 2)
    hook("two")
    relay(0, 1, False)
    hook("three")
    wires.arrive(("m", 1, 3), full(1, 3, 1), mate())
    wires.arrive(("m", 1, 1), full(1, 1, 1), mate())
    hook("sides")
    last(0, 0)
    last(0, 1)
    wires.arrive(("m", 1, 2), full(1, 2, 1), mate())
    hook("far")


def scatter(wires, out, bufs, produce, hook):
    z_half, z_full, mate0, mate1, e_half, e_full = bufs
    rows = out[0].shape[2]
    low, high = pl.ds(0, rows // 2), pl.ds(rows // 2, rows // 2)
    ways = ((0, 1, low, 1), (1, 3, high, -1))
    f32 = jnp.float32

    def wide(ref):
        return ref[...].astype(f32)

    def add_to(ref, *others):
        total = wide(ref)
        for other in others:
            total = total + wide(other)
        ref[...] = total.astype(ref.dtype)

    def mate_send(dz):
        wires.start(("m1", dz), out[1].at[dz, 1], mate1.at[dz], mate())

    def mate_join(dz):
        wires.arrive(("m1", dz), mate1.at[dz], mate())
        add_to(out[1].at[dz, 0], mate1.at[dz])

    produce(1, (2,))
    mate_send(2)
    produce(0, (2,))
    for m in (1, 0):
        for way, dz, part, step in ways:
            wires.start(("a", way, m), out[0].at[2, m, part], z_half.at[way, m], along_z(step))
    produce(0, (1, 3))
    produce(1, (1, 3))
    mate_send(1)
    mate_send(3)
    mate_join(2)
    for way, dz, part, step in ways:
        wires.start(("e", way), out[1].at[2, 0, part], e_half.at[way], along_z(step))
    for m in (1, 0):
        for way, dz, part, step in ways:
            wires.arrive(("a", way, m), z_half.at[way, m], along_z(-step))
            add_to(out[0].at[dz, m, part], z_half.at[way, m])
            wires.start(("b", way, m), out[0].at[dz, m], z_full.at[way, m], along_z(step))
    produce(1, (0,))
    mate_send(0)
    produce(0, (0,))
    hook("early")
    for way, dz, part, step in ways:
        mate_join(dz)
        wires.arrive(("e", way), e_half.at[way], along_z(-step))
        add_to(out[1].at[dz, 0, part], e_half.at[way])
        wires.start(("f", way), out[1].at[dz, 0], e_full.at[way], along_z(step))
    hook("middle")
    for way, dz, part, step in ways:
        wires.arrive(("b", way, 1), z_full.at[way, 1], along_z(-step))
    add_to(out[0].at[0, 1], z_full.at[0, 1], z_full.at[1, 1])
    wires.start(("m0",), out[0].at[0, 1], mate0, mate())
    hook("late")
    for way, dz, part, step in ways:
        wires.arrive(("b", way, 0), z_full.at[way, 0], along_z(-step))
    first = wide(out[0].at[0, 0]) + wide(z_full.at[0, 0]) + wide(z_full.at[1, 0])
    wires.arrive(("m1", 0), mate1.at[0], mate())
    second = wide(out[1].at[0, 0]) + wide(mate1.at[0])
    for way, dz, part, step in ways:
        wires.arrive(("f", way), e_full.at[way], along_z(-step))
        second = second + wide(e_full.at[way])
    wires.arrive(("m0",), mate0, mate())
    first = first + wide(mate0)
    return first, second


def norm_halves(rows, gain):
    mean_square = jnp.mean(rows * rows, axis=-1, keepdims=True)
    normed = (rows * lax.rsqrt(mean_square + EPSILON) * gain).astype(jnp.bfloat16)
    width, _ = column_halves(rows.shape[1])
    return normed[:, :width], normed[:, width:]


def stacked(blocks, h, dzs):
    _, _, rows, width = blocks[h].shape
    parts = [blocks[h][dz].reshape(2 * rows, width) for dz in dzs]
    return parts[0] if len(parts) == 1 else jnp.concatenate(parts, axis=0)


def project_kernel(
    tokens_ref, gain_ref, cos_ref, sin_ref, wq_hbm, wkv_hbm, wo_hbm, q_ref, kv_ref, wo_other,
    weights, others, blocks0, blocks1, load_sems, send_sems, recv_sems,
):
    blocks, rows = (blocks0, blocks1), blocks0.shape[2]
    split, width = blocks0.shape[3], weights.shape[0]
    neighbours = greet()
    qcols = wq_hbm.shape[1]
    cols = qcols + wkv_hbm.shape[1]
    z, x, _, _ = place()
    loads = [
        pltpu.make_async_copy(wq_hbm, weights.at[:, pl.ds(0, qcols)], load_sems.at[0]),
        pltpu.make_async_copy(wkv_hbm, weights.at[:, pl.ds(qcols, cols - qcols)], load_sems.at[1]),
    ]
    for load in loads:
        load.start()
    blocks0[0, 0], blocks1[0, 0] = norm_halves(tokens_ref[...].astype(jnp.float32), gain_ref[...])
    meet(neighbours)
    wires = Wires(send_sems, recv_sems)
    fetch_q = Fetch(wires, "q", wq_hbm, others, False, 0)
    fetch_kv = Fetch(wires, "kv", wkv_hbm, others, False, qcols)
    fetch_o = Fetch(wires, "o", wo_hbm, wo_other, True)

    def emit(dzs, mine):
        shard = weights if mine else others
        part = sum(
            jnp.dot(
                stacked(blocks, h, dzs),
                shard[slice(0, split) if h == 0 else slice(split, width), :],
                preferred_element_type=jnp.float32,
            )
            for h in range(2)
        )
        is_key = (x % 2 == 0) if mine else (x % 2 == 1)
        which = x % 2 if mine else 1 - x % 2
        first_col = 0 if mine else qcols
        for i, dz in enumerate(dzs):
            for m in range(2):
                whole = part[(2 * i + m) * rows : (2 * i + m + 1) * rows]
                zz = (z + dz) % SIDE
                mm = x // 2 if m == 0 else 1 - x // 2
                cosine, sine = cos_ref[zz, mm], sin_ref[zz, mm]
                for head in range(qcols // HEAD_DIM):
                    piece = whole[:, head * HEAD_DIM : (head + 1) * HEAD_DIM]
                    turned = piece * cosine + pltpu.roll(piece, HEAD_DIM // 2, 1) * sine
                    at = first_col + head * HEAD_DIM
                    q_ref[zz, mm, :, at : at + HEAD_DIM] = turned.astype(jnp.bfloat16)
                piece = whole[:, qcols:]
                turned = piece * cosine + pltpu.roll(piece, HEAD_DIM // 2, 1) * sine
                kv_ref[which, zz, mm] = jnp.where(is_key, turned, piece).astype(jnp.bfloat16)

    def hook(name):
        if name == "sent":
            for fetch in (fetch_q, fetch_kv, fetch_o):
                fetch.ask()
        elif name == "one":
            fetch_q.relay()
            fetch_kv.relay()
            for load in loads:
                load.wait()
        elif name == "own pair":
            emit((0,), True)
        elif name == "two":
            fetch_q.pass_on()
        elif name == "three":
            fetch_kv.pass_on()
            fetch_o.relay()
            fetch_q.settle()
        elif name == "sides":
            emit((3, 1), True)
            fetch_kv.settle()
            fetch_q.finish()
            fetch_kv.finish()
            emit((0,), False)
            emit((3, 1), False)
            fetch_o.pass_on()
        else:
            emit((2,), True)
            emit((2,), False)
            fetch_o.settle()
            fetch_o.finish()

    gather(wires, blocks, hook)
    wires.drain()


def project(tokens, gain, cosine, sine, w_query, w_keyval, w_out):
    rows, width = tokens.shape
    cols = w_query.shape[1] + w_keyval.shape[1]
    vmem = pl.BlockSpec(memory_space=pltpu.VMEM)
    hbm = pl.BlockSpec(memory_space=pl.ANY)
    bf16 = jnp.bfloat16
    return pl.pallas_call(
        project_kernel,
        out_shape=(
            jax.ShapeDtypeStruct((SIDE, 2, rows, 2 * w_query.shape[1]), bf16),
            jax.ShapeDtypeStruct((2, SIDE, 2, rows, w_keyval.shape[1]), bf16),
            jax.ShapeDtypeStruct(w_out.shape, bf16),
        ),
        in_specs=[vmem] * 4 + [hbm] * 3,
        out_specs=(vmem, vmem, hbm),
        scratch_shapes=[
            pltpu.VMEM((width, cols), bf16),
            pltpu.VMEM((width, cols), bf16),
            *[pltpu.VMEM((SIDE, 2, rows, part), bf16) for part in column_halves(width)],
            pltpu.SemaphoreType.DMA((2,)),
            pltpu.SemaphoreType.DMA((64,)),
            pltpu.SemaphoreType.DMA((64,)),
        ],
        compiler_params=pltpu.CompilerParams(
            collective_id=0, has_side_effects=True, vmem_limit_bytes=48 << 20
        ),
        name="project",
    )(tokens, gain, cosine, sine, w_query, w_keyval, w_out)


def finish_kernel(
    tokens_ref, attn_ref, gain_ref, wo_hbm, wo2_hbm, wg_hbm, wu_hbm, wd_hbm, out_ref,
    wo, wg, wu, wd, wg2, wu2, wd2, blocks0, blocks1, hidden, hidden2, sending0, sending1,
    z_half, z_full, mate0, mate1, e_half, e_full, state, load_sems, send_sems, recv_sems,
):
    blocks, sending = (blocks0, blocks1), (sending0, sending1)
    _, _, rows, split = blocks0.shape
    width = wo.shape[1]
    neighbours = greet()
    own = wo_hbm.shape[0]
    z, x, _, _ = place()
    loads = [
        pltpu.make_async_copy(src, dst, load_sems.at[i])
        for i, (src, dst) in enumerate(
            ((wo_hbm, wo.at[pl.ds(0, own)]), (wo2_hbm, wo.at[pl.ds(own, own)]), (wg_hbm, wg), (wu_hbm, wu), (wd_hbm, wd))
        )
    ]
    for load in loads:
        load.start()
    meet(neighbours)
    bufs = (z_half, z_full, mate0, mate1, e_half, e_full)
    weight_wires = Wires(send_sems.at[3], recv_sems.at[3])
    fetch_g = Fetch(weight_wires, "g", wg_hbm, wg2, True)
    fetch_u = Fetch(weight_wires, "u", wu_hbm, wu2, True)
    fetch_d = Fetch(weight_wires, "d", wd_hbm, wd2, True)
    fetch_g.ask()
    fetch_u.ask()
    loads[0].wait()
    loads[1].wait()

    def columns(h):
        return pl.ds(0, split) if h == 0 else pl.ds(split, width - split)

    def keep(h, dzs, part):
        for i, dz in enumerate(dzs):
            piece = part[2 * i * rows : 2 * (i + 1) * rows].astype(jnp.bfloat16)
            sending[h][dz] = piece.reshape(2, rows, piece.shape[1])

    def project_out(h, dzs):
        mine, other = x // 2, 1 - x // 2
        left = [attn_ref[(z + dz) % SIDE, m] for dz in dzs for m in (mine, other)]
        left = jnp.concatenate(left, axis=0)
        keep(h, dzs, jnp.dot(left, wo[:, columns(h)], preferred_element_type=jnp.float32))

    def hook_out(name):
        if name == "early":
            fetch_g.relay()
        elif name == "late":
            fetch_u.relay()
            fetch_g.pass_on()

    out_wires = Wires(send_sems.at[0], recv_sems.at[0])
    first, second = scatter(out_wires, sending, bufs, project_out, hook_out)
    for h, proj in enumerate((first, second)):
        state[:, columns(h)] = (tokens_ref[:, columns(h)].astype(jnp.float32) + proj).astype(jnp.bfloat16)
    blocks0[0, 0], blocks1[0, 0] = norm_halves(state[...].astype(jnp.float32), gain_ref[...])

    def gated(dzs, mine):
        gates, ups, result = (wg, wu, hidden) if mine else (wg2, wu2, hidden2)
        gate = upward = 0.0
        for h in range(2):
            left = stacked(blocks, h, dzs)
            across = (((1,), (1,)), ((), ()))
            gate = gate + lax.dot_general(left, gates[:, columns(h)], across, preferred_element_type=jnp.float32)
            upward = upward + lax.dot_general(left, ups[:, columns(h)], across, preferred_element_type=jnp.float32)
        value = (gate / (1.0 + jnp.exp(-gate)) * upward).astype(jnp.bfloat16)
        for i, dz in enumerate(dzs):
            result[dz] = value[2 * i * rows : 2 * (i + 1) * rows].reshape(2, rows, value.shape[1])

    def hook_gated(name):
        if name == "sent":
            fetch_d.ask()
            loads[2].wait()
            loads[3].wait()
        elif name == "one":
            fetch_g.settle()
            fetch_u.pass_on()
        elif name == "own pair":
            gated((0,), True)
            fetch_d.relay()
        elif name == "two":
            fetch_g.finish()
            fetch_u.settle()
        elif name == "sides":
            gated((3, 1), True)
            fetch_d.pass_on()
            fetch_u.finish()
            gated((0,), False)
            gated((3, 1), False)
        elif name == "far":
            gated((2,), True)
            gated((2,), False)
            fetch_d.settle()
            fetch_d.finish()
            loads[4].wait()

    gather_wires = Wires(send_sems.at[1], recv_sems.at[1])
    gather(gather_wires, blocks, hook_gated)
    out_wires.drain()

    def project_down(h, dzs):
        part = 0.0
        for values, weights in ((hidden, wd), (hidden2, wd2)):
            left = [values[dz].reshape(2 * rows, values.shape[3]) for dz in dzs]
            left = left[0] if len(left) == 1 else jnp.concatenate(left, axis=0)
            part = part + jnp.dot(left, weights[:, columns(h)], preferred_element_type=jnp.float32)
        keep(h, dzs, part)

    down_wires = Wires(send_sems.at[2], recv_sems.at[2])
    down = scatter(down_wires, sending, bufs, project_down, lambda name: None)
    for h in range(2):
        out_ref[:, columns(h)] = (state[:, columns(h)].astype(jnp.float32) + down[h]).astype(jnp.bfloat16)
    for wires in (gather_wires, down_wires, weight_wires):
        wires.drain()


def finish(tokens, attn, gain, w_out, w_out_other, w_gate, w_up, w_down):
    rows, width = tokens.shape
    hidden = w_gate.shape[0]
    vmem = pl.BlockSpec(memory_space=pltpu.VMEM)
    hbm = pl.BlockSpec(memory_space=pl.ANY)
    wide, narrow = column_halves(width)
    bf16 = jnp.bfloat16
    return pl.pallas_call(
        finish_kernel,
        out_shape=jax.ShapeDtypeStruct((rows, width), bf16),
        in_specs=[vmem] * 3 + [hbm] * 5,
        out_specs=vmem,
        scratch_shapes=[
            pltpu.VMEM((2 * w_out.shape[0], width), bf16),
            *[pltpu.VMEM((hidden, width), bf16)] * 6,
            pltpu.VMEM((SIDE, 2, rows, wide), bf16),
            pltpu.VMEM((SIDE, 2, rows, narrow), bf16),
            pltpu.VMEM((SIDE, 2, rows, hidden), bf16),
            pltpu.VMEM((SIDE, 2, rows, hidden), bf16),
            pltpu.VMEM((SIDE, 2, rows, wide), bf16),
            pltpu.VMEM((SIDE, 2, rows, narrow), bf16),
            pltpu.VMEM((2, 2, rows // 2, wide), bf16),
            pltpu.VMEM((2, 2, rows, wide), bf16),
            pltpu.VMEM((rows, wide), bf16),
            pltpu.VMEM((SIDE, rows, narrow), bf16),
            pltpu.VMEM((2, rows // 2, narrow), bf16),
            pltpu.VMEM((2, rows, narrow), bf16),
            pltpu.VMEM((rows, width), bf16),
            pltpu.SemaphoreType.DMA((5,)),
            pltpu.SemaphoreType.DMA((4, 48)),
            pltpu.SemaphoreType.DMA((4, 48)),
        ],
        compiler_params=pltpu.CompilerParams(
            collective_id=1, has_side_effects=True, vmem_limit_bytes=60 << 20
        ),
        name="finish",
    )(tokens, attn, gain, w_out, w_out_other, w_gate, w_up, w_down)


def serve_kernel(q_ref, own_ref, first_ref, spot_ref, o_ref, held, peak, total, summed, send_sems, recv_sems):
    z, x, y, core = place()
    mine = lax.rem(lax.div(x + 1, 2), 2)
    theirs = 1 - mine
    base = 1 - core
    rows = q_ref.shape[2]
    width = own_ref.shape[4]
    heads = q_ref.shape[3] // width
    factor = math.log2(math.e) / math.sqrt(width)
    across, ahead, other_core = holder(), along_y(1), twin()
    neighbours = greet()
    held[base, mine] = own_ref[...]
    meet(neighbours)
    started = []

    def send(g, c, target, device):
        made = pltpu.make_async_remote_copy(
            src_ref=held.at[g, c],
            dst_ref=held.at[target, c],
            send_sem=send_sems.at[len(started)],
            recv_sem=recv_sems.at[target, c],
            device_id=device,
            device_id_type=MESH,
        )
        made.start()
        started.append(True)

    def arrive(g, c):
        pltpu.make_async_remote_copy(
            src_ref=held.at[g, c],
            dst_ref=held.at[g, c],
            send_sem=send_sems.at[0],
            recv_sem=recv_sems.at[g, c],
            device_id=across,
            device_id_type=MESH,
        ).wait_recv()

    send(base, mine, base, across)
    send(base, mine, base + 2, ahead)
    send(base, mine, base, other_core)
    peak[...] = jnp.full(peak.shape, NEGATIVE, jnp.float32)
    total[...] = jnp.zeros(total.shape, jnp.float32)
    summed[...] = jnp.zeros(summed.shape, jnp.float32)

    in_run = lax.broadcasted_iota(jnp.int32, (1, 2 * rows), 1)
    later = (in_run >= rows).astype(jnp.int32)

    def column(ref, zz):
        return jnp.concatenate([ref[zz]] * heads, axis=0)

    def step(tiles, g, c, back, causal):
        run = 2 * rows
        shift = (back - 2 * y - core) * (SIDE * SIDE * rows)
        held_before = [(peak[zz], total[zz], summed[zz]) for zz, _, _ in tiles]
        scored = []
        for zz, begin, size in tiles:
            tile = [q_ref[zz, :, :, h * width : (h + 1) * width].reshape(run, width) for h in range(heads)]
            query = jnp.concatenate(tile, axis=0)
            keys = held[g, c, 0, begin : begin + size].reshape(size * run, width)
            scored.append(
                lax.dot_general(query, keys, (((1,), (1,)), ((), ())), preferred_element_type=jnp.float32)
            )
        after = []
        for (zz, begin, size), scores, (old, sums, outs) in zip(tiles, scored, held_before):
            low, high = column(first_ref, zz) + shift, column(spot_ref, zz) + shift
            parts = []
            for run_at in range(size):
                spots = in_run + c * (rows - 2 * rows * later) + later * (SIDE - 2) * rows
                spots = spots + (begin + run_at) * (SIDE * rows)
                seen = spots >= low
                if causal:
                    seen = seen & (spots <= high)
                parts.append(jnp.where(seen, scores[:, run_at * run : (run_at + 1) * run], NEGATIVE))
            top = functools.reduce(jnp.maximum, parts)
            new = jnp.maximum(old, jnp.broadcast_to(jnp.max(top, axis=1, keepdims=True) * factor, old.shape))
            decay = jnp.exp2(old - new)
            parts = [jnp.exp2(part * factor - new) for part in parts]
            weights = jnp.concatenate([part.astype(jnp.bfloat16) for part in parts], axis=1)
            values = held[g, c, 1, begin : begin + size].reshape(size * run, width)
            outs = outs * decay + jnp.dot(weights, values, preferred_element_type=jnp.float32)
            after.append((new, sums * decay + functools.reduce(jnp.add, parts), outs))
        for (zz, _, _), state in zip(tiles, after):
            peak[zz], total[zz], summed[zz] = state

    def own_block(c):
        for pair in ((0, 3), (1, 2)):
            step([(zz, 0, zz + 1) for zz in pair], base, c, 0, True)

    def far_block(c):
        for pair in ((0, 3), (1, 2)):
            step([(zz, zz, SIDE - zz) for zz in pair], base + 4, c, 4, False)

    def per_class(work):
        def one(i, carry):
            work(mine + i * (theirs - mine))
            return carry

        return one

    def first_class(i, carry):
        @pl.when(i == 1)
        def _():
            arrive(base, theirs)
            send(base, theirs, base, other_core)
            arrive(base + 2, mine)
            send(base + 2, mine, base + 4, ahead)
            send(base + 2, mine, base + 2, across)
            send(base + 2, mine, base + 2, other_core)

        own_block(mine + i * (theirs - mine))
        return carry

    lax.fori_loop(0, 2, first_class, 0)

    def middle(stage, carry):
        final = lax.div(stage, 4)
        back = (1 - final) * (1 + lax.rem(stage, 2)) + 3 * final
        c = mine + ((1 - final) * lax.div(stage, 2) + final * (stage - 4)) * (theirs - mine)

        @pl.when(stage == 2)
        def _():
            arrive(base + 2, theirs)
            send(base + 2, theirs, base + 2, other_core)
            arrive(base + 4, mine)
            send(base + 4, mine, base + 4, across)
            send(base + 4, mine, base + 4, other_core)

        @pl.when(stage == 4)
        def _():
            arrive(base + 4, theirs)
            send(base + 4, theirs, base + 4, other_core)

        @pl.when(back != 2)
        def _():
            arrive(base + back, c)

        def over_runs(pair, inner):
            step([(2 * pair + i, 0, SIDE) for i in range(2)], base + back, c, back, False)
            return inner

        return lax.fori_loop(0, SIDE // 2, over_runs, carry)

    lax.fori_loop(0, 6, middle, 0)
    lax.fori_loop(0, 2, per_class(far_block), 0)
    spare = core * 5
    arrive(spare, 0)
    arrive(spare, 1)
    for zz in range(SIDE):
        answer = (summed[zz] / jnp.sum(total[zz], axis=1, keepdims=True)).astype(jnp.bfloat16)
        for h in range(heads):
            piece = answer[h * 2 * rows : (h + 1) * 2 * rows]
            o_ref[zz, :, :, h * width : (h + 1) * width] = piece.reshape(2, rows, width)
    for number in range(len(started)):
        pltpu.make_async_remote_copy(
            src_ref=held.at[0, 0],
            dst_ref=held.at[0, 0],
            send_sem=send_sems.at[number],
            recv_sem=recv_sems.at[0, 0],
            device_id=across,
            device_id_type=MESH,
        ).wait_send()


def serve(queries, own, first, spots):
    rows = queries.shape[2]
    width = own.shape[4]
    heads = queries.shape[3] // width
    tall = heads * 2 * rows
    vmem = pl.BlockSpec(memory_space=pltpu.VMEM)
    return pl.pallas_call(
        serve_kernel,
        out_shape=jax.ShapeDtypeStruct(queries.shape, jnp.bfloat16),
        in_specs=[vmem] * 4,
        out_specs=vmem,
        scratch_shapes=[
            pltpu.VMEM((6, 2, *own.shape), jnp.bfloat16),
            pltpu.VMEM((SIDE, tall, 2 * rows), jnp.float32),
            pltpu.VMEM((SIDE, tall, 2 * rows), jnp.float32),
            pltpu.VMEM((SIDE, tall, width), jnp.float32),
            pltpu.SemaphoreType.DMA((11,)),
            pltpu.SemaphoreType.DMA((6, 2)),
        ],
        compiler_params=pltpu.CompilerParams(
            collective_id=2, has_side_effects=True, vmem_limit_bytes=40 << 20
        ),
        name="serve",
    )(queries, own, first, spots)


def body(tokens, doc_lengths, attn_gain, mlp_gain, w_query, w_keyval, w_out, w_gate, w_up, w_down):
    token_index = lax.axis_index("token")
    x = lax.axis_index("tensor") % SIDE
    rows = tokens.shape[0]
    qblk = 2 * rows
    block_rows = rows * SIDE * SIDE
    outer = (x == 0) | (x == SIDE - 1)
    lows, highs = jnp.where(outer, 0, 1), jnp.where(outer, SIDE - 1, SIDE - 2)
    runs = token_index * block_rows + jnp.arange(SIDE, dtype=jnp.int32) * (SIDE * rows)
    blocks = runs[:, None] + jnp.stack([lows, highs])[None, :] * rows
    spots = (blocks[:, :, None] + jnp.arange(rows, dtype=jnp.int32)).reshape(-1).astype(jnp.int32)
    ends = jnp.cumsum(doc_lengths)
    passed = spots[:, None] >= ends[None, :-1]
    first = jnp.max(jnp.where(passed, ends[None, :-1], 0), axis=1).astype(jnp.int32)
    position = (spots - first).astype(jnp.float32)
    half = HEAD_DIM // 2
    freq = jnp.exp(-math.log(ROPE_BASE) * jnp.arange(half, dtype=jnp.float32) * (2.0 / HEAD_DIM))
    angle = position[:, None] * freq[None, :]
    cosine, sine = jnp.cos(angle), jnp.sin(angle)
    cosine = jnp.concatenate([cosine, cosine], axis=1).reshape(SIDE, 2, rows, HEAD_DIM)
    sine = jnp.concatenate([-sine, sine], axis=1).reshape(SIDE, 2, rows, HEAD_DIM)
    queries, own, w_out_other = project(tokens, attn_gain[None, :], cosine, sine, w_query, w_keyval, w_out)
    attn = serve(queries, own, first.reshape(SIDE, qblk, 1), spots.reshape(SIDE, qblk, 1))
    return finish(tokens, attn, mlp_gain[None, :], w_out, w_out_other, w_gate.T, w_up.T, w_down)


def solution(mesh):
    return jax.shard_map(
        body,
        mesh=mesh,
        in_specs=(
            P(("token", "tensor"), None),
            P(),
            P(),
            P(),
            P(None, "tensor"),
            P(None, "tensor"),
            P("tensor", None),
            P(None, "tensor"),
            P(None, "tensor"),
            P("tensor", None),
        ),
        out_specs=P(("token", "tensor"), None),
        check_vma=False,
    )
```

profile of v0, /device:TPU:0, one launch (start us, length us, event | category | flops | bytes accessed | tf_op | source)
XLA Modules:
  0.0 191.4 jit_solution(8039353387571271069)
XLA Ops:
  0.0 0.0 copy-start.3
  0.0 0.1 add_multiply_fusion
  0.1 0.9 reduce-window.4
  1.0 0.1 broadcast_add_fusion.1
  1.1 0.1 add.84
  1.2 0.1 iota_add_fusion
  1.2 0.1 add.81
  1.3 0.1 select_reduce_fusion
  1.4 0.1 reduce_max.12
  1.5 0.1 subtract_convert_fusion
  1.6 0.1 add.78
  1.6 0.2 add.87
  1.9 0.1 broadcast_add_fusion.spot_ref
  1.9 0.1 copy.17.first_ref
  2.1 1.0 fusion
  3.1 0.2 pad_maximum_fusion
  3.3 0.0 copy-done.3
  3.3 0.0 copy-start.1
  3.3 1.0 copy-done.1
  4.4 0.0 copy-start.4
  4.4 0.7 copy-done.4
  5.1 47.2 %project.1 = (bf16[4,2,64,512]{3,2,1,0:T(8,128)(2,1)S(1)}, bf16[2,4,2,64,128]{4,3,2,1,0:T(8,128)(2,1)S(1)}, bf16[256,4096]{1,0:T(8,128)(2,1)S(1)}) custom-call(bf16[64,4096]{1,0:T(8,128)(2,1)S(1)} %copy-done.1, f32[1,4096]{1,0:T(1,128)S(1)} %bitcast.10, f32[4,2,64,128]{3,2,1,0:T(8,128)S(1)} %get-tuple-element.14.cos_ref, ...), custom_call_target="tpu_custom_call" | custom-call | tf_op jit(solution)/shard_map/project/pallas_call | solution.py:378
  52.3 0.0 copy-start
  52.3 1.3 copy-done
  53.6 31.3 %serve.1.attn_ref = bf16[4,2,64,512]{3,2,1,0:T(8,128)(2,1)S(1)} custom-call(bf16[4,2,64,512]{3,2,1,0:T(8,128)(2,1)S(1)} %get-tuple-element.8.q_ref, bf16[2,4,2,64,128]{4,3,2,1,0:T(8,128)(2,1)S(1)} %get-tuple-element.9.own_ref, s32[4,128,1]{2,1,0:T(8,128)S(1)} %copy.17.first_ref, s32[4,128,1]{2,1,0:T(8,128)S(1)} %broadcast_add_fusion.spot_ref), custom_call_target="tpu_custom_call" | custom-call | tf_op jit(solution)/shard_map/serve/pallas_call | solution.py:726
  85.0 0.0 copy-start.2
  85.0 0.8 copy-done.2
  85.8 103.7 %finish.1 = bf16[64,4096]{1,0:T(8,128)(2,1)} custom-call(bf16[64,4096]{1,0:T(8,128)(2,1)} %tokens_ref.3, bf16[4,2,64,512]{3,2,1,0:T(8,128)(2,1)} %copy-done.2, f32[1,4096]{1,0:T(1,128)} %bitcast.14, bf16[256,4096]{1,0:T(8,128)(2,1)} %wo_hbm.3, bf16[256,4096]{1,0:T(8,128)(2,1)} %copy-done, bf16[448,4096]{1,0:T(8,128)(2,1)} %bitcast.11, ...), custom_call_target="tpu_custom_call" | custom-call | tf_op jit(solution)/shard_map/finish/pallas_call | solution.py:525
  189.5 1.9 copy.19
  (4 shorter events, 0.0 us)
Async XLA Ops:
  0.0 3.3 %copy-start.3 = (bf16[4096,128]{1,0:T(8,128)(2,1)S(1)}, bf16[4096,128]{1,0:T(8,128)(2,1)}, u32[]{:S(2)}) copy-start(bf16[4096,128]{1,0:T(8,128)(2,1)} %wkv_hbm.1) | copy-start | bytes 3145732
  3.3 1.0 copy-start.1
  4.4 0.7 copy-start.4
  52.3 1.3 copy-start
  85.0 0.8 copy-start.2
where the time goes:
time: 194 us; the launch traced here: 191 us
  Pallas kernels  182 us (94%)
  local copies, waits for them, and re-layouts  6.43 us (3%)
  other arithmetic  2.58 us (1%)
    pallas_call x1, Pallas kernels, finish(): pl.pallas_call(finish_kernel, out_shape=jax.ShapeDtypeStruct((rows, width...  104 us
    pallas_call x1, Pallas kernels, project(): pl.pallas_call(project_kernel, out_shape=(jax.ShapeDtypeStruct((SIDE, 2,...  47.2 us
    pallas_call x1, Pallas kernels, serve(): pl.pallas_call(serve_kernel, out_shape=jax.ShapeDtypeStruct(queries.shape...  31.3 us
    unnamed x11, local copies, waits for them, and re-layouts  5.74 us

commit v1 on v0

--- a/solution.py
+++ b/solution.py
@@ -95,9 +95,19 @@
 
 
 class Fetch:
-    def __init__(self, wires, name, src, dst, lanes, first_lane=0):
+    def __init__(self, wires, name, src, dst, lanes, first_lane=0, landed=None, landed_sem=None):
         self.wires, self.name, self.src, self.dst, self.lanes, self.first_lane = wires, name, src, dst, lanes, first_lane
-        self.size = src.shape[1 if lanes else 0] // (YS * CORES)
+        self.landed, self.kept = landed, None
+        if landed is not None:
+            self.kept = pltpu.make_async_copy(landed, self.dst_slot(dst), landed_sem)
+
+    @property
+    def size(self):
+        return self.src.shape[1 if self.lanes else 0] // (YS * CORES)
+
+    def dst_slot(self, ref):
+        _, _, y, core = place()
+        return self.cut(ref, y * CORES + core, None, self.first_lane)
 
     def cut(self, ref, number, part, offset):
         size = self.size if part is None else self.size // 2
@@ -122,11 +132,18 @@
         _, _, y, core = place()
         self.wires.start((self.name, "x"), self.cut(self.src, y * CORES + core, None, 0), self.slot(0, 0), holder())
 
+    def land(self, landed):
+        self.wires.start((self.name, "x"), self.dst_slot(self.src), landed, holder())
+
     def relay(self):
-        self.arrive("x", self.slot(0, 0))
-        self.start("y3", self.slot(0, 0), along_y(1))
-        self.start("y1", self.slot(0, 0), along_y(-1))
-        self.start("c0", self.slot(0, 0), twin())
+        source = self.landed
+        if source is None:
+            source = self.slot(0, 0)
+            self.arrive("x", source)
+        else:
+            self.kept.start()
+        for key, device in (("y3", along_y(1)), ("y1", along_y(-1)), ("c0", twin())):
+            self.wires.start((self.name, key), source, self.slot(0, 0), device)
 
     def pass_on(self):
         self.arrive("y3", self.slot(3, 0))
@@ -144,6 +161,8 @@
     def finish(self):
         for dy in (0, 3, 1, 2):
             self.arrive("c%d" % dy, self.slot(dy, 1))
+        if self.kept is not None:
+            self.kept.wait()
 
 
 def gather(wires, blocks, hook):
@@ -230,6 +249,7 @@
     for m in (1, 0):
         for way, dz, part, step in ways:
             wires.start(("a", way, m), out[0].at[2, m, part], z_half.at[way, m], along_z(step))
+    hook("begun")
     produce(0, (1, 3))
     produce(1, (1, 3))
     mate_send(1)
@@ -284,7 +304,7 @@
 
 
 def project_kernel(
-    tokens_ref, gain_ref, cos_ref, sin_ref, wq_hbm, wkv_hbm, wo_hbm, q_ref, kv_ref, wo_other,
+    tokens_ref, gain_ref, cos_ref, sin_ref, wq_hbm, wkv_hbm, wo_hbm, wg_hbm, q_ref, kv_ref, landed_o, landed_g,
     weights, others, blocks0, blocks1, load_sems, send_sems, recv_sems,
 ):
     blocks, rows = (blocks0, blocks1), blocks0.shape[2]
@@ -304,7 +324,8 @@
     wires = Wires(send_sems, recv_sems)
     fetch_q = Fetch(wires, "q", wq_hbm, others, False, 0)
     fetch_kv = Fetch(wires, "kv", wkv_hbm, others, False, qcols)
-    fetch_o = Fetch(wires, "o", wo_hbm, wo_other, True)
+    fetch_o = Fetch(wires, "o", wo_hbm, None, True)
+    fetch_g = Fetch(wires, "g", wg_hbm, None, True)
 
     def emit(dzs, mine):
         shard = weights if mine else others
@@ -336,8 +357,10 @@
 
     def hook(name):
         if name == "sent":
-            for fetch in (fetch_q, fetch_kv, fetch_o):
-                fetch.ask()
+            fetch_q.ask()
+            fetch_kv.ask()
+            fetch_o.land(landed_o)
+            fetch_g.land(landed_g)
         elif name == "one":
             fetch_q.relay()
             fetch_kv.relay()
@@ -349,7 +372,6 @@
             fetch_q.pass_on()
         elif name == "three":
             fetch_kv.pass_on()
-            fetch_o.relay()
             fetch_q.settle()
         elif name == "sides":
             emit((3, 1), True)
@@ -358,18 +380,17 @@
             fetch_kv.finish()
             emit((0,), False)
             emit((3, 1), False)
-            fetch_o.pass_on()
         else:
             emit((2,), True)
             emit((2,), False)
-            fetch_o.settle()
-            fetch_o.finish()
 
     gather(wires, blocks, hook)
+    wires.arrive(("o", "x"), landed_o, holder())
+    wires.arrive(("g", "x"), landed_g, holder())
     wires.drain()
 
 
-def project(tokens, gain, cosine, sine, w_query, w_keyval, w_out):
+def project(tokens, gain, cosine, sine, w_query, w_keyval, w_out, w_gate):
     rows, width = tokens.shape
     cols = w_query.shape[1] + w_keyval.shape[1]
     vmem = pl.BlockSpec(memory_space=pltpu.VMEM)
@@ -380,10 +401,11 @@
         out_shape=(
             jax.ShapeDtypeStruct((SIDE, 2, rows, 2 * w_query.shape[1]), bf16),
             jax.ShapeDtypeStruct((2, SIDE, 2, rows, w_keyval.shape[1]), bf16),
-            jax.ShapeDtypeStruct(w_out.shape, bf16),
+            jax.ShapeDtypeStruct((w_out.shape[0], w_out.shape[1] // (YS * CORES)), bf16),
+            jax.ShapeDtypeStruct((w_gate.shape[0], w_gate.shape[1] // (YS * CORES)), bf16),
         ),
-        in_specs=[vmem] * 4 + [hbm] * 3,
-        out_specs=(vmem, vmem, hbm),
+        in_specs=[vmem] * 4 + [hbm] * 4,
+        out_specs=(vmem, vmem, hbm, hbm),
         scratch_shapes=[
             pltpu.VMEM((width, cols), bf16),
             pltpu.VMEM((width, cols), bf16),
@@ -396,11 +418,11 @@
             collective_id=0, has_side_effects=True, vmem_limit_bytes=48 << 20
         ),
         name="project",
-    )(tokens, gain, cosine, sine, w_query, w_keyval, w_out)
+    )(tokens, gain, cosine, sine, w_query, w_keyval, w_out, w_gate)
 
 
 def finish_kernel(
-    tokens_ref, attn_ref, gain_ref, wo_hbm, wo2_hbm, wg_hbm, wu_hbm, wd_hbm, out_ref,
+    tokens_ref, attn_ref, gain_ref, wo_hbm, wo2_hbm, wg_hbm, wu_hbm, wd_hbm, landed_g, out_ref,
     wo, wg, wu, wd, wg2, wu2, wd2, blocks0, blocks1, hidden, hidden2, sending0, sending1,
     z_half, z_full, mate0, mate1, e_half, e_full, state, load_sems, send_sems, recv_sems,
 ):
@@ -416,16 +438,14 @@
             ((wo_hbm, wo.at[pl.ds(0, own)]), (wo2_hbm, wo.at[pl.ds(own, own)]), (wg_hbm, wg), (wu_hbm, wu), (wd_hbm, wd))
         )
     ]
-    for load in loads:
+    for load in loads[:2]:
         load.start()
     meet(neighbours)
     bufs = (z_half, z_full, mate0, mate1, e_half, e_full)
     weight_wires = Wires(send_sems.at[3], recv_sems.at[3])
-    fetch_g = Fetch(weight_wires, "g", wg_hbm, wg2, True)
+    fetch_g = Fetch(weight_wires, "g", wg_hbm, wg2, True, 0, landed_g, load_sems.at[5])
     fetch_u = Fetch(weight_wires, "u", wu_hbm, wu2, True)
     fetch_d = Fetch(weight_wires, "d", wd_hbm, wd2, True)
-    fetch_g.ask()
-    fetch_u.ask()
     loads[0].wait()
     loads[1].wait()
 
@@ -444,11 +464,18 @@
         keep(h, dzs, jnp.dot(left, wo[:, columns(h)], preferred_element_type=jnp.float32))
 
     def hook_out(name):
-        if name == "early":
+        if name == "begun":
+            for load in loads[2:]:
+                load.start()
             fetch_g.relay()
+            fetch_u.ask()
+            fetch_d.ask()
+        elif name == "early":
+            fetch_g.pass_on()
+            fetch_u.relay()
         elif name == "late":
-            fetch_u.relay()
-            fetch_g.pass_on()
+            fetch_g.settle()
+            fetch_d.relay()
 
     out_wires = Wires(send_sems.at[0], recv_sems.at[0])
     first, second = scatter(out_wires, sending, bufs, project_out, hook_out)
@@ -470,28 +497,25 @@
 
     def hook_gated(name):
         if name == "sent":
-            fetch_d.ask()
             loads[2].wait()
             loads[3].wait()
+            fetch_u.pass_on()
         elif name == "one":
-            fetch_g.settle()
-            fetch_u.pass_on()
+            fetch_g.finish()
+            fetch_d.pass_on()
         elif name == "own pair":
             gated((0,), True)
-            fetch_d.relay()
-        elif name == "two":
-            fetch_g.finish()
             fetch_u.settle()
+        elif name == "three":
+            fetch_d.settle()
         elif name == "sides":
             gated((3, 1), True)
-            fetch_d.pass_on()
             fetch_u.finish()
             gated((0,), False)
             gated((3, 1), False)
         elif name == "far":
             gated((2,), True)
             gated((2,), False)
-            fetch_d.settle()
             fetch_d.finish()
             loads[4].wait()
 
@@ -515,7 +539,7 @@
         wires.drain()
 
 
-def finish(tokens, attn, gain, w_out, w_out_other, w_gate, w_up, w_down):
+def finish(tokens, attn, gain, w_out, w_out_other, w_gate, w_up, w_down, landed_g):
     rows, width = tokens.shape
     hidden = w_gate.shape[0]
     vmem = pl.BlockSpec(memory_space=pltpu.VMEM)
@@ -525,7 +549,7 @@
     return pl.pallas_call(
         finish_kernel,
         out_shape=jax.ShapeDtypeStruct((rows, width), bf16),
-        in_specs=[vmem] * 3 + [hbm] * 5,
+        in_specs=[vmem] * 3 + [hbm] * 6,
         out_specs=vmem,
         scratch_shapes=[
             pltpu.VMEM((2 * w_out.shape[0], width), bf16),
@@ -543,7 +567,7 @@
             pltpu.VMEM((2, rows // 2, narrow), bf16),
             pltpu.VMEM((2, rows, narrow), bf16),
             pltpu.VMEM((rows, width), bf16),
-            pltpu.SemaphoreType.DMA((5,)),
+            pltpu.SemaphoreType.DMA((6,)),
             pltpu.SemaphoreType.DMA((4, 48)),
             pltpu.SemaphoreType.DMA((4, 48)),
         ],
@@ -551,10 +575,13 @@
             collective_id=1, has_side_effects=True, vmem_limit_bytes=60 << 20
         ),
         name="finish",
-    )(tokens, attn, gain, w_out, w_out_other, w_gate, w_up, w_down)
-
-
-def serve_kernel(q_ref, own_ref, first_ref, spot_ref, o_ref, held, peak, total, summed, send_sems, recv_sems):
+    )(tokens, attn, gain, w_out, w_out_other, w_gate, w_up, w_down, landed_g)
+
+
+def serve_kernel(
+    q_ref, own_ref, first_ref, spot_ref, wo_hbm, landed_o, o_ref, wo_other,
+    held, peak, total, summed, send_sems, recv_sems, weight_send, weight_recv, landed_sem,
+):
     z, x, y, core = place()
     mine = lax.rem(lax.div(x + 1, 2), 2)
     theirs = 1 - mine
@@ -568,6 +595,8 @@
     held[base, mine] = own_ref[...]
     meet(neighbours)
     started = []
+    weight_wires = Wires(weight_send, weight_recv)
+    fetch_o = Fetch(weight_wires, "o", wo_hbm, wo_other, True, 0, landed_o, landed_sem.at[0])
 
     def send(g, c, target, device):
         made = pltpu.make_async_remote_copy(
@@ -667,6 +696,7 @@
         return carry
 
     lax.fori_loop(0, 2, first_class, 0)
+    fetch_o.relay()
 
     def middle(stage, carry):
         final = lax.div(stage, 4)
@@ -696,11 +726,16 @@
 
         return lax.fori_loop(0, SIDE // 2, over_runs, carry)
 
-    lax.fori_loop(0, 6, middle, 0)
+    lax.fori_loop(0, 4, middle, 0)
+    fetch_o.pass_on()
+    lax.fori_loop(4, 6, middle, 0)
+    fetch_o.settle()
     lax.fori_loop(0, 2, per_class(far_block), 0)
     spare = core * 5
     arrive(spare, 0)
     arrive(spare, 1)
+    fetch_o.finish()
+    weight_wires.drain()
     for zz in range(SIDE):
         answer = (summed[zz] / jnp.sum(total[zz], axis=1, keepdims=True)).astype(jnp.bfloat16)
         for h in range(heads):
@@ -717,17 +752,21 @@
         ).wait_send()
 
 
-def serve(queries, own, first, spots):
+def serve(queries, own, first, spots, w_out, landed_o):
     rows = queries.shape[2]
     width = own.shape[4]
     heads = queries.shape[3] // width
     tall = heads * 2 * rows
     vmem = pl.BlockSpec(memory_space=pltpu.VMEM)
+    hbm = pl.BlockSpec(memory_space=pl.ANY)
     return pl.pallas_call(
         serve_kernel,
-        out_shape=jax.ShapeDtypeStruct(queries.shape, jnp.bfloat16),
-        in_specs=[vmem] * 4,
-        out_specs=vmem,
+        out_shape=(
+            jax.ShapeDtypeStruct(queries.shape, jnp.bfloat16),
+            jax.ShapeDtypeStruct(w_out.shape, jnp.bfloat16),
+        ),
+        in_specs=[vmem] * 4 + [hbm] * 2,
+        out_specs=(vmem, hbm),
         scratch_shapes=[
             pltpu.VMEM((6, 2, *own.shape), jnp.bfloat16),
             pltpu.VMEM((SIDE, tall, 2 * rows), jnp.float32),
@@ -735,12 +774,15 @@
             pltpu.VMEM((SIDE, tall, width), jnp.float32),
             pltpu.SemaphoreType.DMA((11,)),
             pltpu.SemaphoreType.DMA((6, 2)),
+            pltpu.SemaphoreType.DMA((12,)),
+            pltpu.SemaphoreType.DMA((12,)),
+            pltpu.SemaphoreType.DMA((1,)),
         ],
         compiler_params=pltpu.CompilerParams(
             collective_id=2, has_side_effects=True, vmem_limit_bytes=40 << 20
         ),
         name="serve",
-    )(queries, own, first, spots)
+    )(queries, own, first, spots, w_out, landed_o)
 
 
 def body(tokens, doc_lengths, attn_gain, mlp_gain, w_query, w_keyval, w_out, w_gate, w_up, w_down):
@@ -754,9 +796,11 @@
     runs = token_index * block_rows + jnp.arange(SIDE, dtype=jnp.int32) * (SIDE * rows)
     blocks = runs[:, None] + jnp.stack([lows, highs])[None, :] * rows
     spots = (blocks[:, :, None] + jnp.arange(rows, dtype=jnp.int32)).reshape(-1).astype(jnp.int32)
-    ends = jnp.cumsum(doc_lengths)
-    passed = spots[:, None] >= ends[None, :-1]
-    first = jnp.max(jnp.where(passed, ends[None, :-1], 0), axis=1).astype(jnp.int32)
+    first = jnp.zeros_like(spots)
+    end = jnp.int32(0)
+    for document in range(doc_lengths.shape[0] - 1):
+        end = end + doc_lengths[document]
+        first = jnp.where(spots >= end, end, first)
     position = (spots - first).astype(jnp.float32)
     half = HEAD_DIM // 2
     freq = jnp.exp(-math.log(ROPE_BASE) * jnp.arange(half, dtype=jnp.float32) * (2.0 / HEAD_DIM))
@@ -764,9 +808,13 @@
     cosine, sine = jnp.cos(angle), jnp.sin(angle)
     cosine = jnp.concatenate([cosine, cosine], axis=1).reshape(SIDE, 2, rows, HEAD_DIM)
     sine = jnp.concatenate([-sine, sine], axis=1).reshape(SIDE, 2, rows, HEAD_DIM)
-    queries, own, w_out_other = project(tokens, attn_gain[None, :], cosine, sine, w_query, w_keyval, w_out)
-    attn = serve(queries, own, first.reshape(SIDE, qblk, 1), spots.reshape(SIDE, qblk, 1))
-    return finish(tokens, attn, mlp_gain[None, :], w_out, w_out_other, w_gate.T, w_up.T, w_down)
+    gates = w_gate.T
+    queries, own, landed_o, landed_g = project(
+        tokens, attn_gain[None, :], cosine, sine, w_query, w_keyval, w_out, gates
+    )
+    first, spots = first.reshape(SIDE, qblk, 1), spots.reshape(SIDE, qblk, 1)
+    attn, w_out_other = serve(queries, own, first, spots, w_out, landed_o)
+    return finish(tokens, attn, mlp_gain[None, :], w_out, w_out_other, gates, w_up.T, w_down, landed_g)
 
 
 def solution(mesh):

time: 194 us -> 183 us (0.943); the launches traced: 191 us -> 183 us
  Pallas kernels: 182 us -> 171 us
    pallas_call x1, Pallas kernels: 47.2 us -> 40.3 us  [project(): pl.pallas_call(project_kernel, out_shape=(jax.ShapeDtypeStruct((SIDE, 2,...]
    pallas_call x1, Pallas kernels: 104 us -> 97.2 us  [finish(): pl.pallas_call(finish_kernel, out_shape=jax.ShapeDtypeStruct((rows, width...]
    unnamed x11 -> x17, local copies, waits for them, and re-layouts: 5.74 us -> 5.75 us
where the time goes in v1:
time: 183 us
  Pallas kernels  171 us (93%)
  local copies, waits for them, and re-layouts  7.51 us (4%)
  other arithmetic  2.83 us (2%)
  between operations  1.97 us (1%)
    pallas_call x1, Pallas kernels, finish(): pl.pallas_call(finish_kernel, out_shape=jax.ShapeDtypeStruct((rows, width...  97.2 us
    pallas_call x1, Pallas kernels, project(): pl.pallas_call(project_kernel, out_shape=(jax.ShapeDtypeStruct((SIDE, 2,...  40.3 us
    pallas_call x1, Pallas kernels, serve(): pl.pallas_call(serve_kernel, out_shape=(jax.ShapeDtypeStruct(queries.shap...  33.1 us
    unnamed x17, local copies, waits for them, and re-layouts  5.75 us

profile of v1, /device:TPU:0, one launch (start us, length us, event | category | flops | bytes accessed | tf_op | source)
XLA Modules:
  0.0 182.9 jit_solution(9841390207634492788)
XLA Ops:
  0.0 0.0 copy-start.4
  0.0 0.1 add_multiply_fusion
  0.1 0.1 broadcast_add_fusion.1
  0.2 0.1 add.89
  0.3 1.4 fusion.3
  3.5 0.6 fusion.2
  4.1 0.1 add.82
  4.2 0.2 add.92
  4.4 0.0 copy-start.1
  4.4 0.8 select_select_fusion
  5.3 1.0 fusion
  6.3 0.2 pad_maximum_fusion
  6.5 0.0 copy-done.4
  6.5 0.0 copy-done.1
  6.5 0.0 copy-start.3
  6.5 1.0 copy-done.3
  7.5 0.0 copy-start.7
  7.5 0.7 copy-done.7
  8.3 0.0 copy-start
  8.3 40.3 %project.1 = (bf16[4,2,64,512]{3,2,1,0:T(8,128)(2,1)S(1)}, bf16[2,4,2,64,128]{4,3,2,1,0:T(8,128)(2,1)S(1)}, bf16[256,512]{1,0:T(8,128)(2,1)S(1)}, bf16[448,512]{1,0:T(8,128)(2,1)S(1)}) custom-call(bf16[64,4096]{1,0:T(8,128)(2,1)S(1)} %copy-done.3, f32[1,4096]{1,0:T(1,128)S(1)} %bitcast.9, f32[4,2,64,128]{3,2,1,0:T(8,128)S(1)} %get-tuple-element.25.cos_ref, ...), custom_call_target="tpu_custom_call" | custom-call | tf_op jit(solution)/shard_map/project/pallas_call | solution.py:399
  48.5 0.0 copy-start.6
  48.5 0.0 copy-done
  48.5 33.1 %serve.1 = (bf16[4,2,64,512]{3,2,1,0:T(8,128)(2,1)S(1)}, bf16[256,4096]{1,0:T(8,128)(2,1)S(1)}) custom-call(bf16[4,2,64,512]{3,2,1,0:T(8,128)(2,1)S(1)} %get-tuple-element.11.q_ref, bf16[2,4,2,64,128]{4,3,2,1,0:T(8,128)(2,1)S(1)} %get-tuple-element.12.own_ref, s32[4,128,1]{2,1,0:T(8,128)S(1)} %get-tuple-element.17.first_ref, ...), custom_call_target="tpu_custom_call" | custom-call | tf_op jit(solution)/shard_map/serve/pallas_call | solution.py:762
  81.6 0.0 copy-done.6
  81.6 0.0 copy-start.2
  81.6 1.3 copy-done.2
  83.0 0.0 copy-start.5
  83.0 0.8 copy-done.5
  83.7 97.2 %finish.1 = bf16[64,4096]{1,0:T(8,128)(2,1)} custom-call(bf16[64,4096]{1,0:T(8,128)(2,1)} %tokens_ref.3, bf16[4,2,64,512]{3,2,1,0:T(8,128)(2,1)} %copy-done.5, f32[1,4096]{1,0:T(1,128)} %bitcast.13, bf16[256,4096]{1,0:T(8,128)(2,1)} %wo_hbm.5, bf16[256,4096]{1,0:T(8,128)(2,1)} %copy-done.2, bf16[448,4096]{1,0:T(8,128)(2,1)} %bitcast.11, ...), custom_call_target="tpu_custom_call" | custom-call | tf_op jit(solution)/shard_map/finish/pallas_call | solution.py:549
  181.0 1.9 %copy.13 = bf16[64,4096]{1,0:T(8,128)(2,1)} copy(bf16[64,4096]{1,0:T(8,128)(2,1)} %finish.1) | data formatting | bytes 1048576
  (3 shorter events, 0.0 us)
Async XLA Ops:
  0.0 6.5 %copy-start.4 = (bf16[4096,128]{1,0:T(8,128)(2,1)S(1)}, bf16[4096,128]{1,0:T(8,128)(2,1)}, u32[]{:S(2)}) copy-start(bf16[4096,128]{1,0:T(8,128)(2,1)} %wkv_hbm.1) | copy-start | bytes 3145732
  4.4 2.1 %copy-start.1 = (bf16[4096,256]{1,0:T(8,128)(2,1)S(1)}, bf16[4096,256]{1,0:T(8,128)(2,1)}, u32[]{:S(2)}) copy-start(bf16[4096,256]{1,0:T(8,128)(2,1)} %wq_hbm.1) | copy-start | bytes 6291460
  6.5 1.0 copy-start.3
  7.5 0.7 copy-start.7
  8.3 40.3 %copy-start = (bf16[256,4096]{1,0:T(8,128)(2,1)S(1)}, bf16[256,4096]{1,0:T(8,128)(2,1)}, u32[]{:S(2)}) copy-start(bf16[256,4096]{1,0:T(8,128)(2,1)} %wo_hbm.5) | copy-start | bytes 6291460
  48.5 33.1 %copy-start.6 = (bf16[448,512]{1,0:T(8,128)(2,1)}, bf16[448,512]{1,0:T(8,128)(2,1)S(1)}, u32[]{:S(2)}) copy-start(bf16[448,512]{1,0:T(8,128)(2,1)S(1)} %get-tuple-element.16.landed_g) | copy-start | bytes 1376260
  81.6 1.3 copy-start.2
  83.0 0.8 copy-start.5

commit v2 on v1

--- a/solution.py
+++ b/solution.py
@@ -58,6 +58,18 @@
 
 def meet(others):
     pl.semaphore_wait(pltpu.get_barrier_semaphore(), others)
+
+
+def row_class(x):
+    return lax.rem(lax.div(x + 1, 2), 2)
+
+
+def document_start(doc_ref, spots):
+    first, end = jnp.zeros_like(spots), 0
+    for document in range(doc_ref.shape[0] - 1):
+        end = end + doc_ref[document]
+        first = jnp.where(spots >= end, end, first)
+    return first
 
 
 def column_halves(width):
@@ -304,24 +316,43 @@
 
 
 def project_kernel(
-    tokens_ref, gain_ref, cos_ref, sin_ref, wq_hbm, wkv_hbm, wo_hbm, wg_hbm, q_ref, kv_ref, landed_o, landed_g,
-    weights, others, blocks0, blocks1, load_sems, send_sems, recv_sems,
+    tokens_hbm, gain_ref, doc_ref, wq_hbm, wkv_hbm, wo_hbm, wg_hbm, q_ref, kv_ref, landed_o, landed_g,
+    tokens_ref, cos_ref, sin_ref, weights, others, blocks0, blocks1, load_sems, send_sems, recv_sems,
 ):
     blocks, rows = (blocks0, blocks1), blocks0.shape[2]
     split, width = blocks0.shape[3], weights.shape[0]
+    arriving = pltpu.make_async_copy(tokens_hbm, tokens_ref, load_sems.at[2])
+    arriving.start()
     neighbours = greet()
     qcols = wq_hbm.shape[1]
     cols = qcols + wkv_hbm.shape[1]
-    z, x, _, _ = place()
+    z, x, y, core = place()
+    mine, token = row_class(x), y * CORES + core
     loads = [
         pltpu.make_async_copy(wq_hbm, weights.at[:, pl.ds(0, qcols)], load_sems.at[0]),
         pltpu.make_async_copy(wkv_hbm, weights.at[:, pl.ds(qcols, cols - qcols)], load_sems.at[1]),
     ]
     for load in loads:
         load.start()
+    arriving.wait()
     blocks0[0, 0], blocks1[0, 0] = norm_halves(tokens_ref[...].astype(jnp.float32), gain_ref[...])
     meet(neighbours)
     wires = Wires(send_sems, recv_sems)
+
+    def angles(number, carry):
+        run, m = lax.div(number, 2), lax.rem(number, 2)
+        at_x = mine + m * (SIDE - 1 - 2 * mine)
+        shape = (rows, HEAD_DIM)
+        spots = lax.broadcasted_iota(jnp.int32, shape, 0) + ((token * SIDE + run) * SIDE + at_x) * rows
+        position = (spots - document_start(doc_ref, spots)).astype(jnp.float32)
+        lane = lax.broadcasted_iota(jnp.int32, shape, 1)
+        upper = lane >= HEAD_DIM // 2
+        pair = jnp.where(upper, lane - HEAD_DIM // 2, lane).astype(jnp.float32)
+        angle = position * jnp.exp(-math.log(ROPE_BASE) * pair * (2.0 / HEAD_DIM))
+        sine = jnp.sin(angle)
+        cos_ref[number] = jnp.cos(angle)
+        sin_ref[number] = jnp.where(upper, sine, -sine)
+        return carry
     fetch_q = Fetch(wires, "q", wq_hbm, others, False, 0)
     fetch_kv = Fetch(wires, "kv", wkv_hbm, others, False, qcols)
     fetch_o = Fetch(wires, "o", wo_hbm, None, True)
@@ -345,7 +376,7 @@
                 whole = part[(2 * i + m) * rows : (2 * i + m + 1) * rows]
                 zz = (z + dz) % SIDE
                 mm = x // 2 if m == 0 else 1 - x // 2
-                cosine, sine = cos_ref[zz, mm], sin_ref[zz, mm]
+                cosine, sine = cos_ref[2 * zz + mm], sin_ref[2 * zz + mm]
                 for head in range(qcols // HEAD_DIM):
                     piece = whole[:, head * HEAD_DIM : (head + 1) * HEAD_DIM]
                     turned = piece * cosine + pltpu.roll(piece, HEAD_DIM // 2, 1) * sine
@@ -361,6 +392,7 @@
             fetch_kv.ask()
             fetch_o.land(landed_o)
             fetch_g.land(landed_g)
+            lax.fori_loop(0, 2 * SIDE, angles, 0)
         elif name == "one":
             fetch_q.relay()
             fetch_kv.relay()
@@ -390,7 +422,7 @@
     wires.drain()
 
 
-def project(tokens, gain, cosine, sine, w_query, w_keyval, w_out, w_gate):
+def project(tokens, gain, doc_lengths, w_query, w_keyval, w_out, w_gate):
     rows, width = tokens.shape
     cols = w_query.shape[1] + w_keyval.shape[1]
     vmem = pl.BlockSpec(memory_space=pltpu.VMEM)
@@ -404,26 +436,29 @@
             jax.ShapeDtypeStruct((w_out.shape[0], w_out.shape[1] // (YS * CORES)), bf16),
             jax.ShapeDtypeStruct((w_gate.shape[0], w_gate.shape[1] // (YS * CORES)), bf16),
         ),
-        in_specs=[vmem] * 4 + [hbm] * 4,
+        in_specs=[hbm, vmem, pl.BlockSpec(memory_space=pltpu.SMEM)] + [hbm] * 4,
         out_specs=(vmem, vmem, hbm, hbm),
         scratch_shapes=[
+            pltpu.VMEM((rows, width), bf16),
+            pltpu.VMEM((2 * SIDE, rows, HEAD_DIM), jnp.float32),
+            pltpu.VMEM((2 * SIDE, rows, HEAD_DIM), jnp.float32),
             pltpu.VMEM((width, cols), bf16),
             pltpu.VMEM((width, cols), bf16),
             *[pltpu.VMEM((SIDE, 2, rows, part), bf16) for part in column_halves(width)],
-            pltpu.SemaphoreType.DMA((2,)),
+            pltpu.SemaphoreType.DMA((3,)),
             pltpu.SemaphoreType.DMA((64,)),
             pltpu.SemaphoreType.DMA((64,)),
         ],
         compiler_params=pltpu.CompilerParams(
-            collective_id=0, has_side_effects=True, vmem_limit_bytes=48 << 20
+            collective_id=0, has_side_effects=True, vmem_limit_bytes=60 << 20
         ),
         name="project",
-    )(tokens, gain, cosine, sine, w_query, w_keyval, w_out, w_gate)
+    )(tokens, gain, doc_lengths, w_query, w_keyval, w_out, w_gate)
 
 
 def finish_kernel(
-    tokens_ref, attn_ref, gain_ref, wo_hbm, wo2_hbm, wg_hbm, wu_hbm, wd_hbm, landed_g, out_ref,
-    wo, wg, wu, wd, wg2, wu2, wd2, blocks0, blocks1, hidden, hidden2, sending0, sending1,
+    tokens_hbm, attn_hbm, gain_ref, wo_hbm, wo2_hbm, wg_hbm, wu_hbm, wd_hbm, landed_g, out_ref,
+    tokens_ref, attn_ref, wo, wg, wu, wd, wg2, wu2, wd2, blocks0, blocks1, hidden, hidden2, sending0, sending1,
     z_half, z_full, mate0, mate1, e_half, e_full, state, load_sems, send_sems, recv_sems,
 ):
     blocks, sending = (blocks0, blocks1), (sending0, sending1)
@@ -438,9 +473,15 @@
             ((wo_hbm, wo.at[pl.ds(0, own)]), (wo2_hbm, wo.at[pl.ds(own, own)]), (wg_hbm, wg), (wu_hbm, wu), (wd_hbm, wd))
         )
     ]
-    for load in loads[:2]:
+    arriving = [
+        pltpu.make_async_copy(attn_hbm, attn_ref, load_sems.at[6]),
+        pltpu.make_async_copy(tokens_hbm, tokens_ref, load_sems.at[7]),
+    ]
+    for load in arriving[:1] + loads[:2] + arriving[1:]:
         load.start()
     meet(neighbours)
+    for load in arriving:
+        load.wait()
     bufs = (z_half, z_full, mate0, mate1, e_half, e_full)
     weight_wires = Wires(send_sems.at[3], recv_sems.at[3])
     fetch_g = Fetch(weight_wires, "g", wg_hbm, wg2, True, 0, landed_g, load_sems.at[5])
@@ -549,9 +590,11 @@
     return pl.pallas_call(
         finish_kernel,
         out_shape=jax.ShapeDtypeStruct((rows, width), bf16),
-        in_specs=[vmem] * 3 + [hbm] * 6,
+        in_specs=[hbm] * 2 + [vmem] + [hbm] * 6,
         out_specs=vmem,
         scratch_shapes=[
+            pltpu.VMEM((rows, width), bf16),
+            pltpu.VMEM(attn.shape, bf16),
             pltpu.VMEM((2 * w_out.shape[0], width), bf16),
             *[pltpu.VMEM((hidden, width), bf16)] * 6,
             pltpu.VMEM((SIDE, 2, rows, wide), bf16),
@@ -567,7 +610,7 @@
             pltpu.VMEM((2, rows // 2, narrow), bf16),
             pltpu.VMEM((2, rows, narrow), bf16),
             pltpu.VMEM((rows, width), bf16),
-            pltpu.SemaphoreType.DMA((6,)),
+            pltpu.SemaphoreType.DMA((8,)),
             pltpu.SemaphoreType.DMA((4, 48)),
             pltpu.SemaphoreType.DMA((4, 48)),
         ],
@@ -579,11 +622,11 @@
 
 
 def serve_kernel(
-    q_ref, own_ref, first_ref, spot_ref, wo_hbm, landed_o, o_ref, wo_other,
-    held, peak, total, summed, send_sems, recv_sems, weight_send, weight_recv, landed_sem,
+    q_ref, own_ref, doc_ref, wo_hbm, landed_o, o_ref, wo_other,
+    first_ref, spot_ref, held, peak, total, summed, send_sems, recv_sems, weight_send, weight_recv, landed_sem,
 ):
     z, x, y, core = place()
-    mine = lax.rem(lax.div(x + 1, 2), 2)
+    mine = row_class(x)
     theirs = 1 - mine
     base = 1 - core
     rows = q_ref.shape[2]
@@ -630,8 +673,16 @@
     in_run = lax.broadcasted_iota(jnp.int32, (1, 2 * rows), 1)
     later = (in_run >= rows).astype(jnp.int32)
 
-    def column(ref, zz):
-        return jnp.concatenate([ref[zz]] * heads, axis=0)
+    def places(zz, carry):
+        row = lax.broadcasted_iota(jnp.int32, first_ref.shape[1:], 0) & (2 * rows - 1)
+        other = (row >= rows).astype(jnp.int32)
+        spots = row + (mine - other + other * (SIDE - 1 - 2 * mine)) * rows
+        spots = spots + ((2 * y + core) * SIDE + zz) * SIDE * rows
+        spot_ref[zz] = spots
+        first_ref[zz] = document_start(doc_ref, spots)
+        return carry
+
+    lax.fori_loop(0, SIDE, places, 0)
 
     def step(tiles, g, c, back, causal):
         run = 2 * rows
@@ -647,7 +698,7 @@
             )
         after = []
         for (zz, begin, size), scores, (old, sums, outs) in zip(tiles, scored, held_before):
-            low, high = column(first_ref, zz) + shift, column(spot_ref, zz) + shift
+            low, high = first_ref[zz] + shift, spot_ref[zz] + shift
             parts = []
             for run_at in range(size):
                 spots = in_run + c * (rows - 2 * rows * later) + later * (SIDE - 2) * rows
@@ -752,7 +803,7 @@
         ).wait_send()
 
 
-def serve(queries, own, first, spots, w_out, landed_o):
+def serve(queries, own, doc_lengths, w_out, landed_o):
     rows = queries.shape[2]
     width = own.shape[4]
     heads = queries.shape[3] // width
@@ -765,9 +816,11 @@
             jax.ShapeDtypeStruct(queries.shape, jnp.bfloat16),
             jax.ShapeDtypeStruct(w_out.shape, jnp.bfloat16),
         ),
-        in_specs=[vmem] * 4 + [hbm] * 2,
+        in_specs=[vmem] * 2 + [pl.BlockSpec(memory_space=pltpu.SMEM)] + [hbm] * 2,
         out_specs=(vmem, hbm),
         scratch_shapes=[
+            pltpu.VMEM((SIDE, tall, 2 * rows), jnp.int32),
+            pltpu.VMEM((SIDE, tall, 2 * rows), jnp.int32),
             pltpu.VMEM((6, 2, *own.shape), jnp.bfloat16),
             pltpu.VMEM((SIDE, tall, 2 * rows), jnp.float32),
             pltpu.VMEM((SIDE, tall, 2 * rows), jnp.float32),
@@ -779,41 +832,18 @@
             pltpu.SemaphoreType.DMA((1,)),
         ],
         compiler_params=pltpu.CompilerParams(
-            collective_id=2, has_side_effects=True, vmem_limit_bytes=40 << 20
+            collective_id=2, has_side_effects=True, vmem_limit_bytes=60 << 20
         ),
         name="serve",
-    )(queries, own, first, spots, w_out, landed_o)
+    )(queries, own, doc_lengths, w_out, landed_o)
 
 
 def body(tokens, doc_lengths, attn_gain, mlp_gain, w_query, w_keyval, w_out, w_gate, w_up, w_down):
-    token_index = lax.axis_index("token")
-    x = lax.axis_index("tensor") % SIDE
-    rows = tokens.shape[0]
-    qblk = 2 * rows
-    block_rows = rows * SIDE * SIDE
-    outer = (x == 0) | (x == SIDE - 1)
-    lows, highs = jnp.where(outer, 0, 1), jnp.where(outer, SIDE - 1, SIDE - 2)
-    runs = token_index * block_rows + jnp.arange(SIDE, dtype=jnp.int32) * (SIDE * rows)
-    blocks = runs[:, None] + jnp.stack([lows, highs])[None, :] * rows
-    spots = (blocks[:, :, None] + jnp.arange(rows, dtype=jnp.int32)).reshape(-1).astype(jnp.int32)
-    first = jnp.zeros_like(spots)
-    end = jnp.int32(0)
-    for document in range(doc_lengths.shape[0] - 1):
-        end = end + doc_lengths[document]
-        first = jnp.where(spots >= end, end, first)
-    position = (spots - first).astype(jnp.float32)
-    half = HEAD_DIM // 2
-    freq = jnp.exp(-math.log(ROPE_BASE) * jnp.arange(half, dtype=jnp.float32) * (2.0 / HEAD_DIM))
-    angle = position[:, None] * freq[None, :]
-    cosine, sine = jnp.cos(angle), jnp.sin(angle)
-    cosine = jnp.concatenate([cosine, cosine], axis=1).reshape(SIDE, 2, rows, HEAD_DIM)
-    sine = jnp.concatenate([-sine, sine], axis=1).reshape(SIDE, 2, rows, HEAD_DIM)
     gates = w_gate.T
     queries, own, landed_o, landed_g = project(
-        tokens, attn_gain[None, :], cosine, sine, w_query, w_keyval, w_out, gates
+        tokens, attn_gain[None, :], doc_lengths, w_query, w_keyval, w_out, gates
     )
-    first, spots = first.reshape(SIDE, qblk, 1), spots.reshape(SIDE, qblk, 1)
-    attn, w_out_other = serve(queries, own, first, spots, w_out, landed_o)
+    attn, w_out_other = serve(queries, own, doc_lengths, w_out, landed_o)
     return finish(tokens, attn, mlp_gain[None, :], w_out, w_out_other, gates, w_up.T, w_down, landed_g)
 
 

time: 183 us -> 176 us (0.962)
  local copies, waits for them, and re-layouts: 7.51 us -> 1.87 us
  Pallas kernels: 171 us -> 174 us
  other arithmetic: 2.83 us -> 0 us
  between operations: 1.97 us -> 0.03 us
    unnamed x17 -> x1, local copies, waits for them, and re-layouts: 5.75 us -> 1.87 us
    pallas_call x1, Pallas kernels: 33.1 us -> 35 us  [serve(): pl.pallas_call(serve_kernel, out_shape=(jax.ShapeDtypeStruct(queries.shap...]
where the time goes in v2:
time: 176 us
  Pallas kernels  174 us (99%)
  local copies, waits for them, and re-layouts  1.87 us (1%)
    pallas_call x1, Pallas kernels, finish(): pl.pallas_call(finish_kernel, out_shape=jax.ShapeDtypeStruct((rows, width...  97 us
    pallas_call x1, Pallas kernels, project(): pl.pallas_call(project_kernel, out_shape=(jax.ShapeDtypeStruct((SIDE, 2,...  42 us
    pallas_call x1, Pallas kernels, serve(): pl.pallas_call(serve_kernel, out_shape=(jax.ShapeDtypeStruct(queries.shap...  35 us

profile of v2, /device:TPU:0, one launch (start us, length us, event | category | flops | bytes accessed | tf_op | source)
XLA Modules:
  0.0 176.0 jit_solution(17282249582334209717)
XLA Ops:
  0.0 42.0 %project.1 = (bf16[4,2,64,512]{3,2,1,0:T(8,128)(2,1)}, bf16[2,4,2,64,128]{4,3,2,1,0:T(8,128)(2,1)}, bf16[256,512]{1,0:T(8,128)(2,1)}, bf16[448,512]{1,0:T(8,128)(2,1)}) custom-call(bf16[64,4096]{1,0:T(8,128)(2,1)} %tokens_hbm.3, f32[1,4096]{1,0:T(1,128)} %bitcast.7, s32[4]{0:T(128)} %doc_ref.3, bf16[4096,256]{1,0:T(8,128)(2,1)} %wq_hbm.1, ...), custom_call_target="tpu_custom_call" | custom-call | tf_op jit(solution)/shard_map/project/pallas_call | solution.py:431
  42.0 35.0 %serve.1 = (bf16[4,2,64,512]{3,2,1,0:T(8,128)(2,1)}, bf16[256,4096]{1,0:T(8,128)(2,1)}) custom-call(bf16[4,2,64,512]{3,2,1,0:T(8,128)(2,1)} %get-tuple-element.11.q_ref, bf16[2,4,2,64,128]{4,3,2,1,0:T(8,128)(2,1)} %get-tuple-element.12.own_ref, s32[4]{0:T(128)} %doc_ref.3, bf16[256,4096]{1,0:T(8,128)(2,1)} %wo_hbm.5, bf16[256,512]{1,0:T(8,128)(2,1)} %get-tuple-element.13.landed_o), custom_call_target="tpu_custom_call" | custom-call | tf_op jit(solution)/shard_map/serve/pallas_call | solution.py:813
  77.0 97.0 %finish.1 = bf16[64,4096]{1,0:T(8,128)(2,1)} custom-call(bf16[64,4096]{1,0:T(8,128)(2,1)} %tokens_hbm.3, bf16[4,2,64,512]{3,2,1,0:T(8,128)(2,1)} %get-tuple-element.14.attn_hbm, f32[1,4096]{1,0:T(1,128)} %bitcast.8, bf16[256,4096]{1,0:T(8,128)(2,1)} %wo_hbm.5, bf16[256,4096]{1,0:T(8,128)(2,1)} %get-tuple-element.15.wo2_hbm, bf16[448,4096]{1,0:T(8,128)(2,1)} %bitcast.5, ...), custom_call_target="tpu_custom_call" | custom-call | tf_op jit(solution)/shard_map/finish/pallas_call | solution.py:590
  174.1 1.9 %copy.12 = bf16[64,4096]{1,0:T(8,128)(2,1)} copy(bf16[64,4096]{1,0:T(8,128)(2,1)} %finish.1) | data formatting | bytes 1048576

commit v3 on v2

--- a/solution.py
+++ b/solution.py
@@ -480,8 +480,7 @@
     for load in arriving[:1] + loads[:2] + arriving[1:]:
         load.start()
     meet(neighbours)
-    for load in arriving:
-        load.wait()
+    arriving[0].wait()
     bufs = (z_half, z_full, mate0, mate1, e_half, e_full)
     weight_wires = Wires(send_sems.at[3], recv_sems.at[3])
     fetch_g = Fetch(weight_wires, "g", wg_hbm, wg2, True, 0, landed_g, load_sems.at[5])
@@ -520,6 +519,7 @@
 
     out_wires = Wires(send_sems.at[0], recv_sems.at[0])
     first, second = scatter(out_wires, sending, bufs, project_out, hook_out)
+    arriving[1].wait()
     for h, proj in enumerate((first, second)):
         state[:, columns(h)] = (tokens_ref[:, columns(h)].astype(jnp.float32) + proj).astype(jnp.bfloat16)
     blocks0[0, 0], blocks1[0, 0] = norm_halves(state[...].astype(jnp.float32), gain_ref[...])
@@ -622,21 +622,27 @@
 
 
 def serve_kernel(
-    q_ref, own_ref, doc_ref, wo_hbm, landed_o, o_ref, wo_other,
-    first_ref, spot_ref, held, peak, total, summed, send_sems, recv_sems, weight_send, weight_recv, landed_sem,
+    q_hbm, own_hbm, doc_ref, wo_hbm, landed_o, o_ref, wo_other,
+    q_ref, first_ref, spot_ref, held, peak, total, summed, send_sems, recv_sems, weight_send, weight_recv, landed_sem,
 ):
     z, x, y, core = place()
     mine = row_class(x)
     theirs = 1 - mine
     base = 1 - core
     rows = q_ref.shape[2]
-    width = own_ref.shape[4]
+    width = own_hbm.shape[4]
     heads = q_ref.shape[3] // width
     factor = math.log2(math.e) / math.sqrt(width)
     across, ahead, other_core = holder(), along_y(1), twin()
     neighbours = greet()
-    held[base, mine] = own_ref[...]
+    loads = [
+        pltpu.make_async_copy(own_hbm, held.at[base, mine], landed_sem.at[1]),
+        pltpu.make_async_copy(q_hbm, q_ref, landed_sem.at[2]),
+    ]
+    for load in loads:
+        load.start()
     meet(neighbours)
+    loads[0].wait()
     started = []
     weight_wires = Wires(weight_send, weight_recv)
     fetch_o = Fetch(weight_wires, "o", wo_hbm, wo_other, True, 0, landed_o, landed_sem.at[0])
@@ -683,6 +689,7 @@
         return carry
 
     lax.fori_loop(0, SIDE, places, 0)
+    loads[1].wait()
 
     def step(tiles, g, c, back, causal):
         run = 2 * rows
@@ -816,9 +823,10 @@
             jax.ShapeDtypeStruct(queries.shape, jnp.bfloat16),
             jax.ShapeDtypeStruct(w_out.shape, jnp.bfloat16),
         ),
-        in_specs=[vmem] * 2 + [pl.BlockSpec(memory_space=pltpu.SMEM)] + [hbm] * 2,
+        in_specs=[hbm] * 2 + [pl.BlockSpec(memory_space=pltpu.SMEM)] + [hbm] * 2,
         out_specs=(vmem, hbm),
         scratch_shapes=[
+            pltpu.VMEM(queries.shape, jnp.bfloat16),
             pltpu.VMEM((SIDE, tall, 2 * rows), jnp.int32),
             pltpu.VMEM((SIDE, tall, 2 * rows), jnp.int32),
             pltpu.VMEM((6, 2, *own.shape), jnp.bfloat16),
@@ -829,7 +837,7 @@
             pltpu.SemaphoreType.DMA((6, 2)),
             pltpu.SemaphoreType.DMA((12,)),
             pltpu.SemaphoreType.DMA((12,)),
-            pltpu.SemaphoreType.DMA((1,)),
+            pltpu.SemaphoreType.DMA((3,)),
         ],
         compiler_params=pltpu.CompilerParams(
             collective_id=2, has_side_effects=True, vmem_limit_bytes=60 << 20

time: 176 us -> 176 us (level)
  no operation moved by 1% of the time
where the time goes in v3:
time: 176 us; the launch traced here: 175 us
  Pallas kernels  174 us (99%)
  local copies, waits for them, and re-layouts  1.87 us (1%)
    pallas_call x1, Pallas kernels, finish(): pl.pallas_call(finish_kernel, out_shape=jax.ShapeDtypeStruct((rows, width...  96.9 us
    pallas_call x1, Pallas kernels, project(): pl.pallas_call(project_kernel, out_shape=(jax.ShapeDtypeStruct((SIDE, 2,...  42 us
    pallas_call x1, Pallas kernels, serve(): pl.pallas_call(serve_kernel, out_shape=(jax.ShapeDtypeStruct(queries.shap...  34.6 us

profile of v3, /device:TPU:0, one launch (start us, length us, event | category | flops | bytes accessed | tf_op | source)
XLA Modules:
  0.0 175.4 jit_solution(588246310337464497)
XLA Ops:
  0.0 42.0 %project.1 = (bf16[4,2,64,512]{3,2,1,0:T(8,128)(2,1)}, bf16[2,4,2,64,128]{4,3,2,1,0:T(8,128)(2,1)}, bf16[256,512]{1,0:T(8,128)(2,1)}, bf16[448,512]{1,0:T(8,128)(2,1)}) custom-call(bf16[64,4096]{1,0:T(8,128)(2,1)} %tokens_hbm.3, f32[1,4096]{1,0:T(1,128)} %bitcast.7, s32[4]{0:T(128)} %doc_ref.3, bf16[4096,256]{1,0:T(8,128)(2,1)} %wq_hbm.1, ...), custom_call_target="tpu_custom_call" | custom-call | tf_op jit(solution)/shard_map/project/pallas_call | solution.py:431
  42.0 34.6 %serve.1 = (bf16[4,2,64,512]{3,2,1,0:T(8,128)(2,1)}, bf16[256,4096]{1,0:T(8,128)(2,1)}) custom-call(bf16[4,2,64,512]{3,2,1,0:T(8,128)(2,1)} %get-tuple-element.11.q_hbm, bf16[2,4,2,64,128]{4,3,2,1,0:T(8,128)(2,1)} %get-tuple-element.12.own_hbm, s32[4]{0:T(128)} %doc_ref.3, bf16[256,4096]{1,0:T(8,128)(2,1)} %wo_hbm.5, bf16[256,512]{1,0:T(8,128)(2,1)} %get-tuple-element.13.landed_o), custom_call_target="tpu_custom_call" | custom-call | tf_op jit(solution)/shard_map/serve/pallas_call | solution.py:820
  76.6 96.9 %finish.1 = bf16[64,4096]{1,0:T(8,128)(2,1)} custom-call(bf16[64,4096]{1,0:T(8,128)(2,1)} %tokens_hbm.3, bf16[4,2,64,512]{3,2,1,0:T(8,128)(2,1)} %get-tuple-element.14.attn_hbm, f32[1,4096]{1,0:T(1,128)} %bitcast.8, bf16[256,4096]{1,0:T(8,128)(2,1)} %wo_hbm.5, bf16[256,4096]{1,0:T(8,128)(2,1)} %get-tuple-element.15.wo2_hbm, bf16[448,4096]{1,0:T(8,128)(2,1)} %bitcast.5, ...), custom_call_target="tpu_custom_call" | custom-call | tf_op jit(solution)/shard_map/finish/pallas_call | solution.py:590
  173.5 1.9 %copy.12 = bf16[64,4096]{1,0:T(8,128)(2,1)} copy(bf16[64,4096]{1,0:T(8,128)(2,1)} %finish.1) | data formatting | bytes 1048576
